TPU v7x, 32 devices: a whole 2x2x4 slice. The times are simulated.
32 devices in a mesh: fsdp: 16 (over z, y, x), tp: 2 (over core).
Axes of the slice: x: 2, y: 2, z: 4, core: 2. Of those that a mesh axis runs over, the one named last changes fastest.
Arguments:
- tokens: bfloat16 [2, 2048, 8192], P(None, 'fsdp', 'tp'), may hold values from -6 to 6
- frozen_weight: bfloat16 [8192, 2048], P('tp', 'fsdp'), may hold values from -0.0625 to 0.0625
- cotangent: bfloat16 [2, 2048, 2048], P(None, 'fsdp'), may hold values from -6 to 6
- block_adapter_index: int32 [2, 16], replicated, may hold values from 0 to 511
- down_weight: bfloat16 [512, 8192, 16], P(None, ('tp', 'fsdp')), may hold values from -0.0625 to 0.0625
- up_weight: bfloat16 [512, 16, 2048], P(None, None, ('tp', 'fsdp')), may hold values from -0.125 to 0.125
Outputs:
- key_value_output: bfloat16 [2, 2048, 2048], P(None, 'fsdp', 'tp')
- input_gradient: bfloat16 [2, 2048, 8192], P(None, 'fsdp', 'tp')
- grad_down: float32 [512, 8192, 16], P(None, ('tp', 'fsdp'))
- up_weight_gradient: float32 [512, 16, 2048], P(None, None, ('tp', 'fsdp'))
Inputs may be any that keep to these rules, and one draw needn't show every extreme that they name: `block_adapter_index`: one adapter for each block of 128 rows of a microbatch.
All inputs are finite; a program needn't handle non-finite values.
Results may differ from a plain program's by a relative error of at most 0.005.
Values may be sent and summed in bfloat16 or wider, within the bound.
No kernel may reach another device: no remote copies, remote signals or barrier semaphores. Data moves between devices by JAX's collectives and lax.ppermute only.
A program may use at most 128 MiB of HBM per device.

v0:
```python
import jax
import jax.numpy as jnp
from jax import lax
from jax.sharding import PartitionSpec as P

BLOCK = 128
adapter_scale = 2.0


def selected_sum(adapter_selector, tiles):
    flat = tiles.reshape(tiles.shape[0], -1)
    return lax.dot_general(
        adapter_selector,
        flat,
        (((0,), (0,)), ((), ())),
        precision=lax.Precision.HIGHEST,
        preferred_element_type=jnp.float32,
    )


def local(tokens, frozen_weight, cotangent, block_adapter_index, down_weight, up_weight):
    microbatch_list, token_block_rows, shard_width = tokens.shape
    kv_width = cotangent.shape[2]
    key_value_slice = kv_width // lax.axis_size("tp")
    row_total = microbatch_list * token_block_rows
    tok_matrix = tokens.reshape(row_total, shard_width)
    cot_matrix = cotangent.reshape(row_total, kv_width)
    adapter_number = down_weight.shape[0]
    rank_width = down_weight.shape[2]
    adapter_range = jnp.arange(adapter_number, dtype=jnp.int32)
    gathered = lax.all_gather(frozen_weight, "fsdp", axis=1, tiled=True)
    kv_partial = jnp.dot(tok_matrix, gathered, preferred_element_type=jnp.float32)
    frozen_key_value = lax.psum_scatter(kv_partial, "tp", scatter_dimension=1, tiled=True)
    frozen_input_gradient = lax.dot_general(
        cot_matrix, gathered, (((1,), (1,)), ((), ())), preferred_element_type=jnp.float32
    )
    cot_slab = lax.dynamic_slice_in_dim(
        cotangent, lax.axis_index("tp") * key_value_slice, key_value_slice, 2
    )
    fsdp_count = lax.axis_size("fsdp")
    per_dev = token_block_rows // BLOCK
    dest_ids = (
        block_adapter_index.reshape(microbatch_list, fsdp_count, per_dev)
        .transpose(1, 0, 2)
        .reshape(fsdp_count, microbatch_list * per_dev)
    )
    down_send = jnp.take(down_weight, dest_ids, axis=0).transpose(0, 1, 3, 2)
    up_send = jnp.take(up_weight, dest_ids, axis=0)
    down_mine, up_mine = (
        lax.all_to_all(down_send, "fsdp", split_axis=0, concat_axis=3, tiled=True),
        lax.all_to_all(up_send, "fsdp", split_axis=0, concat_axis=3, tiled=True),
    )
    down_mine = down_mine.reshape(microbatch_list, per_dev, rank_width, shard_width)
    up_mine = up_mine.reshape(microbatch_list, per_dev, rank_width, key_value_slice)
    tok_blocks = tokens.reshape(microbatch_list, per_dev, BLOCK, shard_width)
    gradient_blocks = cot_slab.reshape(microbatch_list, per_dev, BLOCK, key_value_slice)
    low_part = jnp.einsum(
        "mnbc,mnrc->mnbr", tok_blocks, down_mine, preferred_element_type=jnp.float32
    )
    partial_input_gradient = adapter_scale * jnp.einsum(
        "fsvj,fsyj->fsvy", gradient_blocks, up_mine, preferred_element_type=jnp.float32
    )
    low_sum, back_sum = lax.psum((low_part, partial_input_gradient), "tp")
    low_rank = low_sum.astype(jnp.bfloat16)
    rank_gradient = back_sum.astype(jnp.bfloat16)
    adapter_key_value = (
        adapter_scale
        * jnp.einsum("elui,elis->elus", low_rank, up_mine, preferred_element_type=jnp.float32)
    ).astype(jnp.bfloat16)
    adapter_input_gradient = jnp.einsum(
        "mnbr,mnrc->mnbc", rank_gradient, down_mine, preferred_element_type=jnp.float32
    ).astype(jnp.bfloat16)
    adapter_key_value = adapter_key_value.reshape(
        microbatch_list, token_block_rows, key_value_slice
    )
    adapter_input_gradient = adapter_input_gradient.reshape(
        microbatch_list, token_block_rows, shard_width
    )
    down_tiles = jnp.einsum(
        "mnbc,mnbr->mnrc", tok_blocks, rank_gradient, preferred_element_type=jnp.float32
    )
    up_weight_tiles = adapter_scale * jnp.einsum(
        "puai,puac->puic", low_rank, gradient_blocks, preferred_element_type=jnp.float32
    )
    down_tiles = down_tiles.reshape(microbatch_list * per_dev, rank_width, shard_width)
    up_weight_tiles = up_weight_tiles.reshape(
        microbatch_list * per_dev, rank_width, key_value_slice
    )
    down_owned, up_owned = (
        lax.all_to_all(
            down_tiles.astype(jnp.bfloat16), "fsdp", split_axis=2, concat_axis=0, tiled=True
        ).astype(down_tiles.dtype),
        lax.all_to_all(
            up_weight_tiles.astype(jnp.bfloat16), "fsdp", split_axis=2, concat_axis=0, tiled=True
        ).astype(up_weight_tiles.dtype),
    )
    owned_ids = dest_ids.reshape(-1)
    adapter_selector = (owned_ids[:, None] == adapter_range[None, :]).astype(jnp.float32)
    grad_down = (
        selected_sum(adapter_selector, down_owned)
        .reshape(adapter_number, rank_width, down_weight.shape[1])
        .transpose(0, 2, 1)
    )
    up_weight_gradient = selected_sum(adapter_selector, up_owned).reshape(up_weight.shape)
    key_value_output = (
        frozen_key_value.reshape(microbatch_list, token_block_rows, key_value_slice)
        + adapter_key_value.astype(jnp.float32)
    ).astype(jnp.bfloat16)
    input_gradient = (
        frozen_input_gradient.reshape(microbatch_list, token_block_rows, shard_width)
        + adapter_input_gradient.astype(jnp.float32)
    ).astype(jnp.bfloat16)
    return (key_value_output, input_gradient, grad_down, up_weight_gradient)


def solution(mesh):
    return jax.shard_map(
        local,
        mesh=mesh,
        in_specs=(
            P(None, "fsdp", "tp"),
            P("tp", "fsdp"),
            P(None, "fsdp", None),
            P(),
            P(None, ("tp", "fsdp"), None),
            P(None, None, ("tp", "fsdp")),
        ),
        out_specs=(
            P(None, "fsdp", "tp"),
            P(None, "fsdp", "tp"),
            P(None, ("tp", "fsdp"), None),
            P(None, None, ("tp", "fsdp")),
        ),
        check_vma=False,
    )
```

profile of v0, /device:TPU:0, one launch (start us, length us, event | category | flops | bytes accessed | tf_op | source)
XLA Modules:
  0.0 380.9 jit_solution(13523982944340229810)
XLA Ops:
  8.0 3.8 copy.30
  12.1 2.2 gather_fusion.1
  14.3 248.3 %all-gather.2.cloned.1.call-done = bf16[4096,2048]{1,0:T(8,128)(2,1)} async-done(((bf16[4096,128]{1,0:T(8,128)(2,1)}), bf16[4096,2048]{1,0:T(8,128)(2,1)}) %all-gather.2.cloned.1.call-update) | async-done | bytes 16777232 | tf_op jit(solution)/shard_map/all_gather | solution.py:31
  262.6 9.5 %fusion.36 = f32[256,2048]{1,0:T(8,128)} fusion(bf16[256,4096]{1,0:T(8,128)(2,1)S(1)} %bitcast.91, bf16[4096,2048]{1,0:T(8,128)(2,1)} %all-gather.2.cloned.1.call-done), kind=kOutput, calls=%fused_computation.46 | convolution fusion | flops 4294967296 | bytes 20971520 | tf_op jit(solution)/shard_map/dot_general | solution.py:32
  272.9 3.8 all-to-all-start.1
  276.7 2.9 gather_fusion
  280.5 3.8 all-to-all-done.1
  284.3 3.5 all-to-all-start
  291.5 5.3 %all-to-all-done = bf16[16,2,16,256]{3,2,1,0:T(8,128)(2,1)S(1)} async-done(((bf16[16,2,16,256]{3,2,1,0:T(8,128)(2,1)}), bf16[16,2,16,256]{3,2,1,0:T(8,128)(2,1)S(1)}, u32[]{:S(2)}, u32[]{:S(2)}) %all-to-all-start) | async-done | bytes 262176 | tf_op jit(solution)/shard_map/all_to_all | solution.py:50
  299.4 3.4 all-reduce
  303.4 1.2 reshape.125
  304.6 3.5 all-to-all-start.3
  308.5 3.8 copy.33
  312.3 7.3 %reshape.123 = bf16[16,2,4096]{2,1,0:T(2,128)(2,1)} reshape(bf16[4096,2,16]{2,1,0:T(2,128)(2,1)} %bitcast.93) | data formatting | bytes 524288
  319.7 6.9 %all-to-all-start.2 = ((bf16[16,2,4096]{2,1,0:T(2,128)(2,1)}), bf16[16,2,4096]{2,1,0:T(2,128)(2,1)S(1)}, u32[]{:S(2)}, u32[]{:S(2)}) async-start(bf16[16,2,4096]{2,1,0:T(2,128)(2,1)} %reshape.123), calls=%async_computation.3 | async-start | bytes 524288 | tf_op jit(solution)/shard_map/all_to_all | solution.py:90
  326.6 2.7 fusion.5
  330.3 1.8 fusion.19
  332.2 4.5 %all-to-all-done.2 = bf16[16,2,4096]{2,1,0:T(2,128)(2,1)S(1)} async-done(((bf16[16,2,4096]{2,1,0:T(2,128)(2,1)}), bf16[16,2,4096]{2,1,0:T(2,128)(2,1)S(1)}, u32[]{:S(2)}, u32[]{:S(2)}) %all-to-all-start.2) | async-done | bytes 262176 | tf_op jit(solution)/shard_map/all_to_all | solution.py:90
  336.6 2.4 reshape.124
  339.0 4.4 %copy.34 = bf16[2,16,16,256]{3,1,0,2:T(8,128)(2,1)S(1)} copy(bf16[2,16,16,256]{1,0,3,2:T(2,128)(2,1)} %bitcast.94) | data formatting | bytes 524288 | tf_op jit(solution)/shard_map/all_to_all | solution.py:90
  343.4 1.4 convolution_bitcast_fusion
  344.8 8.3 %copy.39 = f32[512,256,16]{1,2,0:T(8,128)} copy(f32[512,256,16]{1,0,2:T(8,128)S(1)} %convolution_bitcast_fusion) | data formatting | bytes 16777216
  353.1 18.7 %fusion.6 = bf16[2,128,4096]{2,1,0:T(8,128)(2,1)} fusion(f32[2,128,4096]{2,1,0:T(8,128)} %fusion.5, bf16[2,128,2048]{2,1,0:T(8,128)(2,1)S(1)} %copy-done.2, bf16[4096,2048]{1,0:T(8,128)(2,1)} %all-gather.2.cloned.1.call-done), kind=kOutput, calls=%fused_computation.7 | convolution fusion | flops 4297064448 | bytes 24117248 | tf_op jit(solution)/shard_map/dot_general | solution.py:34
  371.7 2.4 fusion.12
  (43 shorter events, 11.0 us)
Async XLA Ops:
  7.2 255.4 %copy-start = (bf16[2,128,4096]{2,1,0:T(8,128)(2,1)S(1)}, bf16[2,128,4096]{2,1,0:T(8,128)(2,1)}, u32[]{:S(2)}) copy-start(bf16[2,128,4096]{2,1,0:T(8,128)(2,1)} %param.6) | copy-start | bytes 6291460
  7.2 4.6 %copy-start.5 = (s32[2,16]{1,0:T(2,128)S(1)}, s32[2,16]{1,0:T(2,128)}, u32[]{:S(2)}) copy-start(s32[2,16]{1,0:T(2,128)} %param.9) | copy-start | bytes 388
  7.2 255.4 %all-gather.2.cloned.1.call-start = ((), (), s32[]{:S(2)}) async-start(), calls=%async_computation.5 | async-start | bytes 17825792 | tf_op jit(solution)/shard_map/all_gather | solution.py:31
  7.9 363.8 %reduce-scatter.2.cloned.1.call-start = ((), (), s32[]{:S(2)}) async-start(), calls=%async_computation.6 | async-start | bytes 3145728 | tf_op jit(solution)/shard_map/reduce_scatter | solution.py:33
  272.9 11.3 %all-to-all-start.1 = ((bf16[16,2,1024]{2,1,0:T(2,128)(2,1)}), bf16[16,2,1024]{2,1,0:T(2,128)(2,1)S(1)}, u32[]{:S(2)}, u32[]{:S(2)}) async-start(bf16[16,2,1024]{2,1,0:T(2,128)(2,1)} %reshape.121), calls=%async_computation.2 | async-start | bytes 131072 | tf_op jit(solution)/shard_map/all_to_all | solution.py:51
  276.7 14.5 %copy-start.1 = (bf16[2,128,2048]{2,1,0:T(8,128)(2,1)S(1)}, bf16[2,128,2048]{2,1,0:T(8,128)(2,1)}, u32[]{:S(2)}) copy-start(bf16[2,128,2048]{2,1,0:T(8,128)(2,1)} %param.8) | copy-start | bytes 3145732
  284.3 4.2 %copy-start.3 = (bf16[16,2,1024]{2,1,0:T(2,128)(2,1)}, bf16[16,2,1024]{2,1,0:T(2,128)(2,1)S(1)}, u32[]{:S(2)}) copy-start(bf16[16,2,1024]{2,1,0:T(2,128)(2,1)S(1)} %all-to-all-done.1) | copy-start | bytes 196612
  284.3 12.6 %all-to-all-start = ((bf16[16,2,16,256]{3,2,1,0:T(8,128)(2,1)}), bf16[16,2,16,256]{3,2,1,0:T(8,128)(2,1)S(1)}, u32[]{:S(2)}, u32[]{:S(2)}) async-start(bf16[16,2,16,256]{3,2,1,0:T(8,128)(2,1)} %select_bitcast_fusion), calls=%async_computation.1 | async-start | bytes 524288 | tf_op jit(solution)/shard_map/all_to_all | solution.py:50
  304.6 15.1 %all-to-all-start.3 = ((bf16[16,2,1024]{2,1,0:T(2,128)(2,1)}), bf16[16,2,1024]{2,1,0:T(2,128)(2,1)S(1)}, u32[]{:S(2)}, u32[]{:S(2)}) async-start(bf16[16,2,1024]{2,1,0:T(2,128)(2,1)} %reshape.125), calls=%async_computation.4 | async-start | bytes 131072 | tf_op jit(solution)/shard_map/all_to_all | solution.py:93
  319.7 16.9 %all-to-all-start.2 = ((bf16[16,2,4096]{2,1,0:T(2,128)(2,1)}), bf16[16,2,4096]{2,1,0:T(2,128)(2,1)S(1)}, u32[]{:S(2)}, u32[]{:S(2)}) async-start(bf16[16,2,4096]{2,1,0:T(2,128)(2,1)} %reshape.123), calls=%async_computation.3 | async-start | bytes 524288 | tf_op jit(solution)/shard_map/all_to_all | solution.py:90
  326.6 3.7 copy-start.4
  344.8 8.3 %copy-start.2 = (bf16[2,128,2048]{2,1,0:T(8,128)(2,1)S(1)}, bf16[2,128,2048]{2,1,0:T(8,128)(2,1)}, u32[]{:S(2)}) copy-start(bf16[2,128,2048]{2,1,0:T(8,128)(2,1)} %param.8) | copy-start | bytes 3145732
Sparse Core Ops, SparseCore 0:
  10.7 251.8 all-gather.1
  272.2 7.8 reduce-scatter.1
where the time goes:
time: 382 us; the launch traced here: 381 us
  waiting for transfers between devices  263 us (69%)
  local copies, waits for them, and re-layouts  44.1 us (12%)
  matrix products  37.8 us (10%)
  starting transfers between devices  17.9 us (5%)
  between operations  14.2 us (4%)
    all_gather x1, waiting for transfers between devices, local(): gathered = lax.all_gather(frozen_weight, 'fsdp', axis=1, tiled=True)  248 us
    unnamed x20, local copies, waits for them, and re-layouts  25.1 us
    dot_general x1, matrix products, local(): lax.dot_general(cot_matrix, gathered, (((1,), (1,)), ((), ())), preferred...  18.7 us
    dot_general x1, matrix products, local(): jnp.dot(tok_matrix, gathered, preferred_element_type=jnp.float32)  9.45 us
  transfers between devices with their start and end apart: 6, of which 4 were waited for; matrix products, arithmetic and copies ran while one was open for 19% of the time, Pallas kernels for 0%

commit v1 on v0

--- a/solution.py
+++ b/solution.py
@@ -28,7 +28,14 @@
     adapter_number = down_weight.shape[0]
     rank_width = down_weight.shape[2]
     adapter_range = jnp.arange(adapter_number, dtype=jnp.int32)
-    gathered = lax.all_gather(frozen_weight, "fsdp", axis=1, tiled=True)
+    count = lax.axis_size("fsdp")
+    hops = [(i, (i + 1) % count) for i in range(count)]
+    parts = [frozen_weight]
+    for hop in range(1, count):
+        parts = [lax.ppermute(parts[0], "fsdp", hops), *parts]
+    full = jnp.concatenate(parts, axis=1)
+    offset = (lax.axis_index("fsdp") + 1) * parts[-1].shape[1]
+    gathered = jnp.roll(full, offset, axis=1)
     kv_partial = jnp.dot(tok_matrix, gathered, preferred_element_type=jnp.float32)
     frozen_key_value = lax.psum_scatter(kv_partial, "tp", scatter_dimension=1, tiled=True)
     frozen_input_gradient = lax.dot_general(

time: 382 us -> 539 us (1.41)
  waiting for transfers between devices: 263 us -> 345 us
  local copies, waits for them, and re-layouts: 44.1 us -> 111 us
  starting transfers between devices: 17.9 us -> 30.8 us
  matrix products: 37.8 us -> 28.9 us
    ppermute x0 -> x15, waiting for transfers between devices: none -> 341 us  [local(): parts = [lax.ppermute(parts[0], 'fsdp', hops), *parts]]
    all_gather x1 -> x0, waiting for transfers between devices: 248 us -> none  [local(): gathered = lax.all_gather(frozen_weight, 'fsdp', axis=1, tiled=True)]
    unnamed x20 -> x99, local copies, waits for them, and re-layouts: 25.1 us -> 93.3 us
    dot_general x1, matrix products: 18.7 us -> 8.45 us  [local(): lax.dot_general(cot_matrix, gathered, (((1,), (1,)), ((), ())), preferred...]
  transfers between devices with their start and end apart: 6 -> 20, of which waited for: 4 -> 15; matrix products, arithmetic and copies ran while one was open for 19% -> 24% of each run, Pallas kernels for 0% -> 0%
where the time goes in v1:
time: 539 us; the launch traced here: 538 us
  waiting for transfers between devices  345 us (64%)
  local copies, waits for them, and re-layouts  111 us (21%)
  starting transfers between devices  30.8 us (6%)
  matrix products  28.9 us (5%)
  between operations  14.4 us (3%)
    ppermute x15, waiting for transfers between devices, local(): parts = [lax.ppermute(parts[0], 'fsdp', hops), *parts]  341 us
    unnamed x99, local copies, waits for them, and re-layouts  93.3 us
  transfers between devices with their start and end apart: 20, of which 15 were waited for; matrix products, arithmetic and copies ran while one was open for 24% of the time, Pallas kernels for 0%

profile of v1, /device:TPU:0, one launch (start us, length us, event | category | flops | bytes accessed | tf_op | source)
XLA Modules:
  0.0 537.7 jit_solution(7147304414484572414)
XLA Ops:
  10.2 27.4 %collective-permute-done = bf16[4096,128]{1,0:T(8,128)(2,1)S(1)} collective-permute-done((bf16[4096,128]{1,0:T(8,128)(2,1)}, bf16[4096,128]{1,0:T(8,128)(2,1)S(1)}, u32[]{:S(2)}, u32[]{:S(2)}) %collective-permute-start) | collective-permute-done | bytes 1048608 | tf_op jit(solution)/shard_map/ppermute | solution.py:35
  38.6 27.9 %collective-permute-done.1 = bf16[4096,128]{1,0:T(8,128)(2,1)S(1)} collective-permute-done((bf16[4096,128]{1,0:T(8,128)(2,1)S(1)}, bf16[4096,128]{1,0:T(8,128)(2,1)S(1)}, u32[]{:S(2)}, u32[]{:S(2)}) %collective-permute-start.1) | collective-permute-done | bytes 1048608 | tf_op jit(solution)/shard_map/ppermute | solution.py:35
  67.4 27.1 %collective-permute-done.2 = bf16[4096,128]{1,0:T(8,128)(2,1)S(1)} collective-permute-done((bf16[4096,128]{1,0:T(8,128)(2,1)S(1)}, bf16[4096,128]{1,0:T(8,128)(2,1)S(1)}, u32[]{:S(2)}, u32[]{:S(2)}) %collective-permute-start.2) | collective-permute-done | bytes 1048608 | tf_op jit(solution)/shard_map/ppermute | solution.py:35
  95.5 26.2 %collective-permute-done.3 = bf16[4096,128]{1,0:T(8,128)(2,1)S(1)} collective-permute-done((bf16[4096,128]{1,0:T(8,128)(2,1)S(1)}, bf16[4096,128]{1,0:T(8,128)(2,1)S(1)}, u32[]{:S(2)}, u32[]{:S(2)}) %collective-permute-start.3) | collective-permute-done | bytes 1048608 | tf_op jit(solution)/shard_map/ppermute | solution.py:35
  122.7 25.3 %collective-permute-done.4 = bf16[4096,128]{1,0:T(8,128)(2,1)S(1)} collective-permute-done((bf16[4096,128]{1,0:T(8,128)(2,1)S(1)}, bf16[4096,128]{1,0:T(8,128)(2,1)S(1)}, u32[]{:S(2)}, u32[]{:S(2)}) %collective-permute-start.4) | collective-permute-done | bytes 1048608 | tf_op jit(solution)/shard_map/ppermute | solution.py:35
  149.0 24.5 %collective-permute-done.5 = bf16[4096,128]{1,0:T(8,128)(2,1)S(1)} collective-permute-done((bf16[4096,128]{1,0:T(8,128)(2,1)S(1)}, bf16[4096,128]{1,0:T(8,128)(2,1)S(1)}, u32[]{:S(2)}, u32[]{:S(2)}) %collective-permute-start.5) | collective-permute-done | bytes 1048608 | tf_op jit(solution)/shard_map/ppermute | solution.py:35
  174.5 23.6 %collective-permute-done.6 = bf16[4096,128]{1,0:T(8,128)(2,1)S(1)} collective-permute-done((bf16[4096,128]{1,0:T(8,128)(2,1)S(1)}, bf16[4096,128]{1,0:T(8,128)(2,1)S(1)}, u32[]{:S(2)}, u32[]{:S(2)}) %collective-permute-start.6) | collective-permute-done | bytes 1048608 | tf_op jit(solution)/shard_map/ppermute | solution.py:35
  199.1 22.8 %collective-permute-done.7 = bf16[4096,128]{1,0:T(8,128)(2,1)S(1)} collective-permute-done((bf16[4096,128]{1,0:T(8,128)(2,1)S(1)}, bf16[4096,128]{1,0:T(8,128)(2,1)S(1)}, u32[]{:S(2)}, u32[]{:S(2)}) %collective-permute-start.7) | collective-permute-done | bytes 1048608 | tf_op jit(solution)/shard_map/ppermute | solution.py:35
  222.9 22.3 %collective-permute-done.8 = bf16[4096,128]{1,0:T(8,128)(2,1)S(1)} collective-permute-done((bf16[4096,128]{1,0:T(8,128)(2,1)S(1)}, bf16[4096,128]{1,0:T(8,128)(2,1)S(1)}, u32[]{:S(2)}, u32[]{:S(2)}) %collective-permute-start.8) | collective-permute-done | bytes 1048608 | tf_op jit(solution)/shard_map/ppermute | solution.py:35
  246.2 22.3 %collective-permute-done.9 = bf16[4096,128]{1,0:T(8,128)(2,1)S(1)} collective-permute-done((bf16[4096,128]{1,0:T(8,128)(2,1)S(1)}, bf16[4096,128]{1,0:T(8,128)(2,1)S(1)}, u32[]{:S(2)}, u32[]{:S(2)}) %collective-permute-start.9) | collective-permute-done | bytes 1048608 | tf_op jit(solution)/shard_map/ppermute | solution.py:35
  269.6 22.3 %collective-permute-done.10 = bf16[4096,128]{1,0:T(8,128)(2,1)S(1)} collective-permute-done((bf16[4096,128]{1,0:T(8,128)(2,1)S(1)}, bf16[4096,128]{1,0:T(8,128)(2,1)S(1)}, u32[]{:S(2)}, u32[]{:S(2)}) %collective-permute-start.10) | collective-permute-done | bytes 1048608 | tf_op jit(solution)/shard_map/ppermute | solution.py:35
  292.9 22.4 %collective-permute-done.11 = bf16[4096,128]{1,0:T(8,128)(2,1)S(1)} collective-permute-done((bf16[4096,128]{1,0:T(8,128)(2,1)S(1)}, bf16[4096,128]{1,0:T(8,128)(2,1)S(1)}, u32[]{:S(2)}, u32[]{:S(2)}) %collective-permute-start.11) | collective-permute-done | bytes 1048608 | tf_op jit(solution)/shard_map/ppermute | solution.py:35
  316.2 22.3 %collective-permute-done.12 = bf16[4096,128]{1,0:T(8,128)(2,1)S(1)} collective-permute-done((bf16[4096,128]{1,0:T(8,128)(2,1)S(1)}, bf16[4096,128]{1,0:T(8,128)(2,1)S(1)}, u32[]{:S(2)}, u32[]{:S(2)}) %collective-permute-start.12) | collective-permute-done | bytes 1048608 | tf_op jit(solution)/shard_map/ppermute | solution.py:35
  339.5 24.1 %collective-permute-done.13 = bf16[4096,128]{1,0:T(8,128)(2,1)} collective-permute-done((bf16[4096,128]{1,0:T(8,128)(2,1)S(1)}, bf16[4096,128]{1,0:T(8,128)(2,1)}, u32[]{:S(2)}, u32[]{:S(2)}) %collective-permute-start.13) | collective-permute-done | bytes 1048608 | tf_op jit(solution)/shard_map/ppermute | solution.py:35
  372.2 7.0 %all-to-all-start.1 = ((bf16[16,2,1024]{2,1,0:T(2,128)(2,1)}), bf16[16,2,1024]{2,1,0:T(2,128)(2,1)S(1)}, u32[]{:S(2)}, u32[]{:S(2)}) async-start(bf16[16,2,1024]{2,1,0:T(2,128)(2,1)} %reshape.124), calls=%async_computation.2 | async-start | bytes 131072 | tf_op jit(solution)/shard_map/all_to_all | solution.py:58
  440.4 6.9 %all-to-all-start = ((bf16[16,2,16,256]{3,2,1,0:T(8,128)(2,1)}), bf16[16,2,16,256]{3,2,1,0:T(8,128)(2,1)S(1)}, u32[]{:S(2)}, u32[]{:S(2)}) async-start(bf16[16,2,16,256]{3,2,1,0:T(8,128)(2,1)} %select_bitcast_fusion), calls=%async_computation.1 | async-start | bytes 524288 | tf_op jit(solution)/shard_map/all_to_all | solution.py:57
  447.3 9.7 %fusion.5 = f32[256,2048]{0,1:T(8,128)} fusion(bf16[256,4096]{1,0:T(8,128)(2,1)S(1)} %bitcast.89, bf16[4096,4096]{1,0:T(8,128)(2,1)} %constant_dynamic-update-slice_fusion, s32[]{:T(128)S(6)} %select_n.38), kind=kOutput, calls=%fused_computation.11 | convolution fusion | flops 4294967296 | bytes 20971524 | tf_op jit(solution)/shard_map/dot_general | solution.py:39
  466.2 6.9 %all-to-all-start.3 = ((bf16[16,2,1024]{2,1,0:T(2,128)(2,1)}), bf16[16,2,1024]{2,1,0:T(2,128)(2,1)S(1)}, u32[]{:S(2)}, u32[]{:S(2)}) async-start(bf16[16,2,1024]{2,1,0:T(2,128)(2,1)} %reshape.128), calls=%async_computation.4 | async-start | bytes 131072 | tf_op jit(solution)/shard_map/all_to_all | solution.py:100
  477.3 7.3 %reshape.126 = bf16[16,2,4096]{2,1,0:T(2,128)(2,1)} reshape(bf16[4096,2,16]{2,1,0:T(2,128)(2,1)} %bitcast.91) | data formatting | bytes 524288
  484.6 6.9 %all-to-all-start.2 = ((bf16[16,2,4096]{2,1,0:T(2,128)(2,1)}), bf16[16,2,4096]{2,1,0:T(2,128)(2,1)S(1)}, u32[]{:S(2)}, u32[]{:S(2)}) async-start(bf16[16,2,4096]{2,1,0:T(2,128)(2,1)} %reshape.126), calls=%async_computation.3 | async-start | bytes 524288 | tf_op jit(solution)/shard_map/all_to_all | solution.py:97
  497.2 4.2 all-to-all-done.2
  503.8 4.4 copy.37
  509.6 8.3 %copy.42 = f32[512,256,16]{1,2,0:T(8,128)} copy(f32[512,256,16]{1,0,2:T(8,128)S(1)} %convolution_bitcast_fusion) | data formatting | bytes 16777216
  517.8 8.4 %fusion = f32[4096,256]{0,1:T(8,128)S(1)} fusion(bf16[256,2048]{1,0:T(8,128)(2,1)} %bitcast.98, bf16[4096,4096]{1,0:T(8,128)(2,1)} %constant_dynamic-update-slice_fusion, s32[]{:T(128)S(6)} %select_n.38), kind=kOutput, calls=%fused_computation.2 | convolution fusion | flops 4294967296 | bytes 22020100 | tf_op jit(solution)/shard_map/dot_general | solution.py:41
  (152 shorter events, 112.5 us)
Async XLA Ops:
  7.2 440.2 %copy-start = (bf16[2,128,4096]{2,1,0:T(8,128)(2,1)S(1)}, bf16[2,128,4096]{2,1,0:T(8,128)(2,1)}, u32[]{:S(2)}) copy-start(bf16[2,128,4096]{2,1,0:T(8,128)(2,1)} %param.6) | copy-start | bytes 6291460
  7.2 411.7 %copy-start.2 = (bf16[4096,128]{1,0:T(8,128)(2,1)S(1)}, bf16[4096,128]{1,0:T(8,128)(2,1)}, u32[]{:S(2)}) copy-start(bf16[4096,128]{1,0:T(8,128)(2,1)} %param.7) | copy-start | bytes 3145732
  7.2 30.4 %collective-permute-start = (bf16[4096,128]{1,0:T(8,128)(2,1)}, bf16[4096,128]{1,0:T(8,128)(2,1)S(1)}, u32[]{:S(2)}, u32[]{:S(2)}) collective-permute-start(bf16[4096,128]{1,0:T(8,128)(2,1)} %param.7), channel_id=1, source_target_pairs={{0,2},{2,4},{4,6},{6,8},{8,10},{10,12},{12,14},{14,16},{16,18},{18... | collective-permute-start | bytes 3145736 | tf_op jit(solution)/shard_map/ppermute | solution.py:35
  38.5 27.9 %collective-permute-start.1 = (bf16[4096,128]{1,0:T(8,128)(2,1)S(1)}, bf16[4096,128]{1,0:T(8,128)(2,1)S(1)}, u32[]{:S(2)}, u32[]{:S(2)}) collective-permute-start(bf16[4096,128]{1,0:T(8,128)(2,1)S(1)} %collective-permute-done), channel_id=1, source_target_pairs={{0,2},{2,4},{4,6},{6,8},{8,10},{10,12},{12,14},{14,16},{16,18},{18... | collective-permute-start | bytes 3145736 | tf_op jit(solution)/shard_map/ppermute | solution.py:35
  67.4 27.1 %collective-permute-start.2 = (bf16[4096,128]{1,0:T(8,128)(2,1)S(1)}, bf16[4096,128]{1,0:T(8,128)(2,1)S(1)}, u32[]{:S(2)}, u32[]{:S(2)}) collective-permute-start(bf16[4096,128]{1,0:T(8,128)(2,1)S(1)} %collective-permute-done.1), channel_id=1, source_target_pairs={{0,2},{2,4},{4,6},{6,8},{8,10},{10,12},{12,14},{14,16},{16,18},{18... | collective-permute-start | bytes 3145736 | tf_op jit(solution)/shard_map/ppermute | solution.py:35
  95.5 26.2 %collective-permute-start.3 = (bf16[4096,128]{1,0:T(8,128)(2,1)S(1)}, bf16[4096,128]{1,0:T(8,128)(2,1)S(1)}, u32[]{:S(2)}, u32[]{:S(2)}) collective-permute-start(bf16[4096,128]{1,0:T(8,128)(2,1)S(1)} %collective-permute-done.2), channel_id=1, source_target_pairs={{0,2},{2,4},{4,6},{6,8},{8,10},{10,12},{12,14},{14,16},{16,18},{18... | collective-permute-start | bytes 3145736 | tf_op jit(solution)/shard_map/ppermute | solution.py:35
  122.7 25.4 %collective-permute-start.4 = (bf16[4096,128]{1,0:T(8,128)(2,1)S(1)}, bf16[4096,128]{1,0:T(8,128)(2,1)S(1)}, u32[]{:S(2)}, u32[]{:S(2)}) collective-permute-start(bf16[4096,128]{1,0:T(8,128)(2,1)S(1)} %collective-permute-done.3), channel_id=1, source_target_pairs={{0,2},{2,4},{4,6},{6,8},{8,10},{10,12},{12,14},{14,16},{16,18},{18... | collective-permute-start | bytes 3145736 | tf_op jit(solution)/shard_map/ppermute | solution.py:35
  149.0 24.5 %collective-permute-start.5 = (bf16[4096,128]{1,0:T(8,128)(2,1)S(1)}, bf16[4096,128]{1,0:T(8,128)(2,1)S(1)}, u32[]{:S(2)}, u32[]{:S(2)}) collective-permute-start(bf16[4096,128]{1,0:T(8,128)(2,1)S(1)} %collective-permute-done.4), channel_id=1, source_target_pairs={{0,2},{2,4},{4,6},{6,8},{8,10},{10,12},{12,14},{14,16},{16,18},{18... | collective-permute-start | bytes 3145736 | tf_op jit(solution)/shard_map/ppermute | solution.py:35
  174.5 23.6 %collective-permute-start.6 = (bf16[4096,128]{1,0:T(8,128)(2,1)S(1)}, bf16[4096,128]{1,0:T(8,128)(2,1)S(1)}, u32[]{:S(2)}, u32[]{:S(2)}) collective-permute-start(bf16[4096,128]{1,0:T(8,128)(2,1)S(1)} %collective-permute-done.5), channel_id=1, source_target_pairs={{0,2},{2,4},{4,6},{6,8},{8,10},{10,12},{12,14},{14,16},{16,18},{18... | collective-permute-start | bytes 3145736 | tf_op jit(solution)/shard_map/ppermute | solution.py:35
  199.1 22.8 %collective-permute-start.7 = (bf16[4096,128]{1,0:T(8,128)(2,1)S(1)}, bf16[4096,128]{1,0:T(8,128)(2,1)S(1)}, u32[]{:S(2)}, u32[]{:S(2)}) collective-permute-start(bf16[4096,128]{1,0:T(8,128)(2,1)S(1)} %collective-permute-done.6), channel_id=1, source_target_pairs={{0,2},{2,4},{4,6},{6,8},{8,10},{10,12},{12,14},{14,16},{16,18},{18... | collective-permute-start | bytes 3145736 | tf_op jit(solution)/shard_map/ppermute | solution.py:35
  222.9 22.3 %collective-permute-start.8 = (bf16[4096,128]{1,0:T(8,128)(2,1)S(1)}, bf16[4096,128]{1,0:T(8,128)(2,1)S(1)}, u32[]{:S(2)}, u32[]{:S(2)}) collective-permute-start(bf16[4096,128]{1,0:T(8,128)(2,1)S(1)} %collective-permute-done.7), channel_id=1, source_target_pairs={{0,2},{2,4},{4,6},{6,8},{8,10},{10,12},{12,14},{14,16},{16,18},{18... | collective-permute-start | bytes 3145736 | tf_op jit(solution)/shard_map/ppermute | solution.py:35
  246.2 22.3 %collective-permute-start.9 = (bf16[4096,128]{1,0:T(8,128)(2,1)S(1)}, bf16[4096,128]{1,0:T(8,128)(2,1)S(1)}, u32[]{:S(2)}, u32[]{:S(2)}) collective-permute-start(bf16[4096,128]{1,0:T(8,128)(2,1)S(1)} %collective-permute-done.8), channel_id=1, source_target_pairs={{0,2},{2,4},{4,6},{6,8},{8,10},{10,12},{12,14},{14,16},{16,18},{18... | collective-permute-start | bytes 3145736 | tf_op jit(solution)/shard_map/ppermute | solution.py:35
  269.6 22.3 %collective-permute-start.10 = (bf16[4096,128]{1,0:T(8,128)(2,1)S(1)}, bf16[4096,128]{1,0:T(8,128)(2,1)S(1)}, u32[]{:S(2)}, u32[]{:S(2)}) collective-permute-start(bf16[4096,128]{1,0:T(8,128)(2,1)S(1)} %collective-permute-done.9), channel_id=1, source_target_pairs={{0,2},{2,4},{4,6},{6,8},{8,10},{10,12},{12,14},{14,16},{16,18},{18... | collective-permute-start | bytes 3145736 | tf_op jit(solution)/shard_map/ppermute | solution.py:35
  292.9 22.4 %collective-permute-start.11 = (bf16[4096,128]{1,0:T(8,128)(2,1)S(1)}, bf16[4096,128]{1,0:T(8,128)(2,1)S(1)}, u32[]{:S(2)}, u32[]{:S(2)}) collective-permute-start(bf16[4096,128]{1,0:T(8,128)(2,1)S(1)} %collective-permute-done.10), channel_id=1, source_target_pairs={{0,2},{2,4},{4,6},{6,8},{8,10},{10,12},{12,14},{14,16},{16,18},{18... | collective-permute-start | bytes 3145736 | tf_op jit(solution)/shard_map/ppermute | solution.py:35
  316.2 22.4 %collective-permute-start.12 = (bf16[4096,128]{1,0:T(8,128)(2,1)S(1)}, bf16[4096,128]{1,0:T(8,128)(2,1)S(1)}, u32[]{:S(2)}, u32[]{:S(2)}) collective-permute-start(bf16[4096,128]{1,0:T(8,128)(2,1)S(1)} %collective-permute-done.11), channel_id=1, source_target_pairs={{0,2},{2,4},{4,6},{6,8},{8,10},{10,12},{12,14},{14,16},{16,18},{18... | collective-permute-start | bytes 3145736 | tf_op jit(solution)/shard_map/ppermute | solution.py:35
  339.5 24.1 %collective-permute-start.13 = (bf16[4096,128]{1,0:T(8,128)(2,1)S(1)}, bf16[4096,128]{1,0:T(8,128)(2,1)}, u32[]{:S(2)}, u32[]{:S(2)}) collective-permute-start(bf16[4096,128]{1,0:T(8,128)(2,1)S(1)} %collective-permute-done.12), channel_id=1, source_target_pairs={{0,2},{2,4},{4,6},{6,8},{8,10},{10,12},{12,14},{14,16},{16,18},{18... | collective-permute-start | bytes 3145736 | tf_op jit(solution)/shard_map/ppermute | solution.py:35
  363.7 19.3 %collective-permute-start.14 = (bf16[4096,128]{1,0:T(8,128)(2,1)}, bf16[4096,128]{1,0:T(8,128)(2,1)}, u32[]{:S(2)}, u32[]{:S(2)}) collective-permute-start(bf16[4096,128]{1,0:T(8,128)(2,1)} %collective-permute-done.13), channel_id=1, source_target_pairs={{0,2},{2,4},{4,6},{6,8},{8,10},{10,12},{12,14},{14,16},{16,18},{18... | collective-permute-start | bytes 3145736 | tf_op jit(solution)/shard_map/ppermute | solution.py:35
  372.2 68.2 %all-to-all-start.1 = ((bf16[16,2,1024]{2,1,0:T(2,128)(2,1)}), bf16[16,2,1024]{2,1,0:T(2,128)(2,1)S(1)}, u32[]{:S(2)}, u32[]{:S(2)}) async-start(bf16[16,2,1024]{2,1,0:T(2,128)(2,1)} %reshape.124), calls=%async_computation.2 | async-start | bytes 131072 | tf_op jit(solution)/shard_map/all_to_all | solution.py:58
  382.1 54.8 %copy-start.6 = (bf16[4096,128]{1,0:T(8,128)(2,1)S(1)}, bf16[4096,128]{1,0:T(8,128)(2,1)}, u32[]{:S(2)}) copy-start(bf16[4096,128]{1,0:T(8,128)(2,1)} %copy-done.5) | copy-start | bytes 3145732
  382.1 55.9 %copy-start.4 = (bf16[4096,128]{1,0:T(8,128)(2,1)S(1)}, bf16[4096,128]{1,0:T(8,128)(2,1)}, u32[]{:S(2)}) copy-start(bf16[4096,128]{1,0:T(8,128)(2,1)} %copy-done.3) | copy-start | bytes 3145732
  440.4 18.6 %all-to-all-start = ((bf16[16,2,16,256]{3,2,1,0:T(8,128)(2,1)}), bf16[16,2,16,256]{3,2,1,0:T(8,128)(2,1)S(1)}, u32[]{:S(2)}, u32[]{:S(2)}) async-start(bf16[16,2,16,256]{3,2,1,0:T(8,128)(2,1)} %select_bitcast_fusion), calls=%async_computation.1 | async-start | bytes 524288 | tf_op jit(solution)/shard_map/all_to_all | solution.py:57
  447.3 80.9 %reduce-scatter.2.cloned.1.call-start = ((), (), s32[]{:S(2)}) async-start(), calls=%async_computation.5 | async-start | bytes 3145728 | tf_op jit(solution)/shard_map/reduce_scatter | solution.py:40
  466.2 18.5 %all-to-all-start.3 = ((bf16[16,2,1024]{2,1,0:T(2,128)(2,1)}), bf16[16,2,1024]{2,1,0:T(2,128)(2,1)S(1)}, u32[]{:S(2)}, u32[]{:S(2)}) async-start(bf16[16,2,1024]{2,1,0:T(2,128)(2,1)} %reshape.128), calls=%async_computation.4 | async-start | bytes 131072 | tf_op jit(solution)/shard_map/all_to_all | solution.py:100
  484.6 16.8 %all-to-all-start.2 = ((bf16[16,2,4096]{2,1,0:T(2,128)(2,1)}), bf16[16,2,4096]{2,1,0:T(2,128)(2,1)S(1)}, u32[]{:S(2)}, u32[]{:S(2)}) async-start(bf16[16,2,4096]{2,1,0:T(2,128)(2,1)} %reshape.126), calls=%async_computation.3 | async-start | bytes 524288 | tf_op jit(solution)/shard_map/all_to_all | solution.py:97
  (26 other events, 591.5 us)
Sparse Core Ops, SparseCore 0:
  457.2 11.0 reduce-scatter.1
